TPU v7x, 32 devices: a whole 2x2x4 slice. The times are simulated.
32 devices in a mesh: dp: 8 (over z, y), mp: 4 (over x, core).
Axes of the slice: x: 2, y: 2, z: 4, core: 2. Of those that a mesh axis runs over, the one named last changes fastest.
Arguments:
- states: bfloat16 [32768, 512], P(('dp', 'mp')), may hold values from -6 to 6
- cotangent: bfloat16 [32768, 512], P(('dp', 'mp')), may hold values from -6 to 6
- halting: int32 [32768], P(('dp', 'mp')), may hold values 0 or 1
- lengths: int32 [16], P('dp'), may hold values from 1 to 2048, 20480 in all
- attention_weights: float32 [4, 512, 512], P(None, 'dp', 'mp'), may hold values from -3 to 3, as said below
- inner_weight: float32 [512, 2048], P('dp', 'mp'), may hold values from -0.25 to 0.25
- outer_weight: float32 [2048, 512], P('dp', 'mp'), may hold values from -0.125 to 0.125
- norm_gains: float32 [2, 512], replicated, may hold values from 0.5 to 1.5
- norm_biases: float32 [2, 512], replicated, may hold values from -3 to 3
- attention_left: float32 [4, 512, 512], P(None, 'dp', 'mp'), may hold values from -5.869539e-07 to 6.836954e-06, as said below
- attention_right: float32 [4, 512, 512], P(None, 'dp', 'mp'), may hold values from -5.869539e-07 to 6.836954e-06, as said below
- inner_left: float32 [512, 512], P('dp', 'mp'), may hold values from -1.17390774e-06 to 2.6173908e-05, as said below
- inner_right: float32 [2048, 2048], P('dp', 'mp'), may hold values from -5.869539e-07 to 6.836954e-06, as said below
- outer_left: float32 [2048, 2048], P('dp', 'mp'), may hold values from -5.869539e-07 to 6.836954e-06, as said below
- outer_right: float32 [512, 512], P('dp', 'mp'), may hold values from -1.17390774e-06 to 2.6173908e-05, as said below
- attention_left_root: float32 [4, 512, 512], P(None, 'dp'), may hold values from -5.3125 to 36.425198, as said below
- attention_right_root: float32 [4, 512, 512], P(None, None, 'mp'), may hold values from -5.3125 to 36.425198, as said below
- inner_left_root: float32 [512, 512], P('dp'), may hold values from -3.7565048 to 25.756505, as said below
- inner_right_root: float32 [2048, 2048], P(None, 'mp'), may hold values from -2.65625 to 33.768948, as said below
- outer_left_root: float32 [2048, 2048], P('dp'), may hold values from -2.65625 to 33.768948, as said below
- outer_right_root: float32 [512, 512], P(None, 'mp'), may hold values from -3.7565048 to 25.756505, as said below
Outputs:
- output_states: bfloat16 [32768, 512], P(('dp', 'mp'))
- states_grad: bfloat16 [32768, 512], P(('dp', 'mp'))
- grad_norm: float32 [], replicated
- attention_grad: float32 [4, 512, 512], P(None, 'dp', 'mp')
- inner_grad: float32 [512, 2048], P('dp', 'mp')
- outer_grad: float32 [2048, 512], P('dp', 'mp')
- norm_grad: float32 [2048], P(('dp', 'mp'))
- attention_new: float32 [4, 512, 512], P(None, 'dp', 'mp')
- inner_new: float32 [512, 2048], P('dp', 'mp')
- outer_new: float32 [2048, 512], P('dp', 'mp')
- norm_new: float32 [2048], P(('dp', 'mp'))
- attention_left_new: float32 [4, 512, 512], P(None, 'dp', 'mp')
- attention_right_new: float32 [4, 512, 512], P(None, 'dp', 'mp')
- inner_left_new: float32 [512, 512], P('dp', 'mp')
- inner_right_new: float32 [2048, 2048], P('dp', 'mp')
- outer_left_new: float32 [2048, 2048], P('dp', 'mp')
- outer_right_new: float32 [512, 512], P('dp', 'mp')
Inputs may be any that keep to these rules, and one draw needn't show every extreme that they name: `lengths`: positions at or beyond a sequence's length are padding; every sequence has at least one real token. `attention_weights`: query, key and value projections, then the output projection. `attention_left`: symmetric. `attention_right`: symmetric. `inner_left`: symmetric. `inner_right`: symmetric. `outer_left`: symmetric. `outer_right`: symmetric. `attention_left_root`: symmetric. `attention_right_root`: symmetric. `inner_left_root`: symmetric. `inner_right_root`: symmetric. `outer_left_root`: symmetric. `outer_right_root`: symmetric.
All inputs are finite; a program needn't handle non-finite values. No bound on the sum of `halting` or of `lengths` on one device may be relied on, other than what follows from the above.
Results may differ from a plain program's by a relative error of at most 0.012.
The roundings to bfloat16 on the way count: a program that leaves them out, or rounds other values in their place, can miss the bound.
Values may be sent and summed in bfloat16 or wider, within the bound.
A program may use at most 192 MiB of HBM per device.

v0:
```python
import functools
import math

import jax
import jax.numpy as jnp
from jax import lax
from jax.experimental import pallas as pl
from jax.experimental.pallas import tpu as pltpu
from jax.sharding import PartitionSpec as P

D = 512
HEADS = 8
DH = 64
FF = 2048
SEQ = 2048
SEQ_GRP = 2
PAIR = 2 * DH
QUERY_ROWS = 256
FORWARD_CHUNKS = 1
KEY_ROWS = 256
FF_PART = 256
TOKEN_ROWS = 512

F32 = jnp.float32
BF16 = jnp.bfloat16
epsilon = 1e-06
step_rate = 1.0
NN = (((1,), (0,)), ((), ()))
NT = (((1,), (1,)), ((), ()))
TN = (((0,), (0,)), ((), ()))
VMEM_LIMIT = 56 * 1024 * 1024
BACKWARD_VMEM = 62 * 1024 * 1024


def mm(left, right, dims=NN):
    return lax.dot_general(left, right, dims, preferred_element_type=F32)


def split2(value):
    high = value.astype(BF16)
    return high, (value - high.astype(F32)).astype(BF16)


def split3(value):
    high = value.astype(BF16).astype(F32)
    rest = value - high
    middle = rest.astype(BF16).astype(F32)
    return high, middle, rest - middle


MESH = pl.DeviceIdType.MESH


class Place:
    def __init__(self, far_count):
        data_rank = lax.axis_index("dp")
        self.far_count = far_count
        self.model = lax.axis_index("mp")
        self.far, self.near = data_rank // 2, data_rank % 2
        self.data_rank = 2 * self.far + self.near
        side, core = self.model // 2, self.model % 2
        self.side, self.core = side, core
        self.beside = 2 * (1 - side) + core
        self.twin = 2 * side + 1 - core
        self.twin_beside = 2 * (1 - side) + 1 - core
        self.to_beside = {"mp": self.beside}
        self.to_twin = {"mp": self.twin}
        self.to_near = {"dp": 2 * self.far + 1 - self.near}

    def other_far(self, step):
        return (self.far + step) % self.far_count

    def to_far(self, step):
        return {"dp": 2 * self.other_far(step) + self.near}

    def meet(self):
        barrier = pltpu.get_barrier_semaphore()
        partners = [self.to_far(step) for step in range(1, self.far_count)]
        partners += [self.to_near, self.to_beside, self.to_twin]
        for partner in partners:
            pl.semaphore_signal(barrier, inc=1, device_id=partner, device_id_type=MESH)
        pl.semaphore_wait(barrier, len(partners))


class Wires:
    def __init__(self, send_sems, recv_sems):
        self.sems = (send_sems, recv_sems)
        self.used = 0

    def copy(self, source, target, partner):
        index = self.used
        self.used += 1
        return pltpu.make_async_remote_copy(
            src_ref=source,
            dst_ref=target,
            send_sem=self.sems[0].at[index],
            recv_sem=self.sems[1].at[index],
            device_id=partner,
            device_id_type=MESH,
        )


def start_all(copies):
    for copy in copies:
        copy.start()


def wait_all(copies):
    for copy in copies:
        copy.wait()


def columns(index, size):
    return pl.ds(pl.multiple_of(index * size, size), size)


class Chunk:
    def __init__(self, rows, cols, row_size, col_size):
        self.rows, self.cols, self.row_size, self.col_size = rows, cols, row_size, col_size

    def columns(self, index):
        offset = pl.multiple_of(index * self.col_size + self.cols[0], math.gcd(self.col_size, max(self.cols[0], 128)))
        return pl.ds(offset, self.cols[1])

    @property
    def row_window(self):
        return pl.ds(*self.rows)

    @property
    def shape(self):
        return self.rows[1], self.cols[1]


def whole_chunk(rows, cols):
    return Chunk((0, rows), (0, cols), rows, cols)


class Staged:
    def __init__(self, active, twin_stage):
        self.active, self.twin_stage = active, twin_stage
        self.stages = []

    def start(self, number):
        copies = self.stages[number]
        if self.active is None:
            start_all(copies)
        elif number != self.twin_stage:
            pl.when(self.active)(lambda: start_all(copies))
        else:
            pl.when(self.sends)(lambda: start_all(copies))

    def wait(self, number):
        copies = self.stages[number]
        if self.active is None:
            wait_all(copies)
        elif number != self.twin_stage:
            pl.when(self.active)(lambda: wait_all(copies))
        else:

            @pl.when(self.sends)
            def _():
                for copy in copies:
                    copy.wait_send()

            @pl.when(jnp.logical_not(self.sends))
            def _():
                for copy in copies:
                    copy.wait_recv()


class Gather(Staged):
    def __init__(self, wires, place, full, order, chunk, active=None):
        super().__init__(active, len(order) - 1)
        self.sends = active
        mine, side = chunk.columns(place.model), chunk.columns(place.beside)
        self.home = full.at[place.far, place.near, chunk.row_window, mine]
        fars, nears, cols = place.far, place.near, [mine]

        def send(col, partner):
            view = full.at[fars, nears, chunk.row_window, col]
            return wires.copy(view, view, partner)

        for letter in order:
            if letter == "x":
                self.stages.append([send(mine, place.to_beside)])
                cols = [mine, side]
            elif letter == "y":
                self.stages.append([send(col, place.to_near) for col in cols])
                nears = slice(None)
            elif letter == "c":
                self.stages.append([send(col, place.to_twin) for col in cols])
            else:
                ways = [place.to_far(step) for step in range(1, place.far_count)]
                self.stages.append([send(col, way) for col in cols for way in ways])
                fars = slice(None)

    def begin(self):
        self.start(0)

    def advance(self, number):
        self.wait(number)
        if number + 1 < len(self.stages):
            self.start(number + 1)


GATHER_STEPS = 4


def gather_copies(far_count):
    return far_count + 6


def reduce_plan(order, far_count, rows, cols):
    slots, nears, fars = 2, 2, far_count
    plan = []
    for letter in order:
        if letter == "x":
            plan.append((letter, slots, nears, fars, (nears, fars, rows, cols)))
            slots = 1
        elif letter == "y":
            plan.append((letter, slots, nears, fars, (slots, fars, rows, cols)))
            nears = 1
        else:
            plan.append((letter, slots, nears, fars, (far_count, slots, nears, rows, cols)))
            fars = 1
    return plan


REDUCE_BUFFERS = 8
REDUCE_STEPS = 4


def reduce_copies(far_count):
    return far_count + 6


def reduce_scratch(order, far_count, rows, cols):
    shape = (2, 2, far_count, rows, cols)
    buffers = [pltpu.VMEM(shape, F32), pltpu.VMEM(shape, BF16)]
    for *_, shape in reduce_plan(order, far_count, rows, cols):
        buffers += [pltpu.VMEM(shape, BF16), pltpu.VMEM(shape, BF16)]
    return buffers


class Reducer(Staged):
    def __init__(self, wires, place, buffers, order, low=None, chunk=None, given=None, active=None):
        super().__init__(active, 0)
        self.sends = None if active is None else jnp.logical_not(active)
        self.place = place
        self.mine = None
        self.acc, self.got = buffers[:2]
        self.out, self.arrived = buffers[2::2], buffers[3::2]
        rows, size = self.acc.shape[-2:]
        self.plan = reduce_plan(order, place.far_count, rows, size)
        self.chunk = chunk
        self.kept = (place.model, place.beside)
        if given is not None:
            first = [wires.copy(given, self.got, place.to_twin)]
        else:
            twins = (place.twin, place.twin_beside)
            first = [
                wires.copy(
                    low.at[:, near, chunk.row_window, chunk.columns(twins[slot])],
                    self.got.at[slot, near],
                    place.to_twin,
                )
                for slot in range(2)
                for near in range(2)
            ]
        self.stages = [first]
        for (letter, *_), out, arrived in zip(self.plan, self.out, self.arrived):
            if letter == "z":
                stage = [
                    wires.copy(out.at[place.other_far(step)], arrived.at[step], place.to_far(step))
                    for step in range(1, place.far_count)
                ]
            else:
                stage = [wires.copy(out, arrived, place.to_beside if letter == "x" else place.to_near)]
            self.stages.append(stage)

    def loads(self, partial, mine, load_sems):
        self.mine = mine
        return [
            pltpu.make_async_copy(
                partial.at[:, near, self.chunk.row_window, self.chunk.columns(self.kept[slot])],
                mine.at[slot, near],
                load_sems.at[2 * slot + near],
            )
            for slot in range(2)
            for near in range(2)
        ]

    def begin(self):
        self.start(0)

    def held(self, number):
        letter, slots, nears, fars, _ = self.plan[number]
        place = self.place
        return (
            letter,
            range(slots),
            range(2) if nears == 2 else (place.near,),
            range(place.far_count) if fars > 1 else (place.far,),
        )

    def prepare(self, number):
        letter, slots, nears, fars = self.held(number)
        place, acc, out = self.place, self.acc, self.out[number]
        if letter == "x":
            for i, near in enumerate(nears):
                for j, far in enumerate(fars):
                    out[i, j] = acc[1, near, far].astype(BF16)
        elif letter == "y":
            for slot in slots:
                for j, far in enumerate(fars):
                    out[slot, j] = acc[slot, 1 - place.near, far].astype(BF16)
        else:
            for slot in slots:
                for i, near in enumerate(nears):
                    for far in fars:
                        out[far, slot, i] = acc[slot, near, far].astype(BF16)

    def absorb(self, number):
        letter, slots, nears, fars = self.held(number)
        place, acc, arrived = self.place, self.acc, self.arrived[number]
        if letter == "x":
            for i, near in enumerate(nears):
                for j, far in enumerate(fars):
                    acc[0, near, far] += arrived[i, j].astype(F32)
        elif letter == "y":
            for slot in slots:
                for j, far in enumerate(fars):
                    acc[slot, place.near, far] += arrived[slot, j].astype(F32)
        else:
            for slot in slots:
                for i, near in enumerate(nears):
                    total = acc[slot, near, place.far]
                    for step in range(1, place.far_count):
                        total = total + arrived[step, slot, i].astype(F32)
                    acc[slot, near, place.far] = total

    def advance(self, number):
        self.wait(number)

        def add():
            if number == 0:
                for slot in range(2):
                    for near in range(2):
                        for far in range(self.place.far_count):
                            spot = (slot, near, far)
                            own = self.acc[spot] if self.mine is None else self.mine[spot].astype(F32)
                            self.acc[spot] = own + self.got[spot].astype(F32)
            else:
                self.absorb(number - 1)
            if number < len(self.plan):
                self.prepare(number)

        if self.active is None:
            add()
        else:
            pl.when(self.active)(add)
        if number < len(self.plan):
            self.start(number + 1)

    def result(self):
        return self.acc[0, self.place.near, self.place.far]


class Spread:
    def __init__(self, wires, place, tile, stages, slots):
        self.place, self.tile, self.stages, self.slots = place, tile, stages, slots
        self.copies = [
            [wires.copy(tile, stages.at[number], partner)]
            for number, partner in enumerate((place.to_twin, place.to_beside, place.to_near))
        ]
        self.copies.append(
            [wires.copy(tile, slots.at[place.far], place.to_far(step)) for step in range(1, place.far_count)]
        )

    def begin(self):
        start_all(self.copies[0])

    def advance(self, number):
        wait_all(self.copies[number])
        if number == 3:
            self.slots[self.place.far] = self.tile[...]
            total = self.slots[0]
            for far in range(1, self.place.far_count):
                total = total + self.slots[far]
            self.tile[...] = total
        else:
            self.tile[...] += self.stages[number]
            start_all(self.copies[number + 1])


def spread_copies(far_count):
    return far_count - 1 + 3


def spread_scratch(far_count, shape):
    return [pltpu.VMEM(shape, F32), pltpu.VMEM((3,) + shape, F32), pltpu.VMEM((far_count,) + shape, F32)]


def any_spec():
    return pl.BlockSpec(memory_space=pl.ANY)


def vmem_spec():
    return pl.BlockSpec(memory_space=pltpu.VMEM)


def smem_spec():
    return pl.BlockSpec(memory_space=pltpu.SMEM)


def own_lanes(parity):
    lane = lax.broadcasted_iota(jnp.int32, (1, PAIR), 1)
    return (lane < DH) if parity == 0 else (lane >= DH)


def lane_in_half():
    return lax.broadcasted_iota(jnp.int32, (1, PAIR), 1) % DH


def blend(parity, own, extra):
    mine = jnp.where(own_lanes(parity), 1.0, 0.0)
    return own * mine.astype(BF16) + extra * (1.0 - mine).astype(BF16)


def slot_calls(step, width, calls):
    def at(sub_step):
        for slot, call in calls:
            if slot % width == sub_step:
                pl.when(step == slot // width)(call)

    return at


PROJECT_ORDERS = ("zxyc", "zyxc")
FORWARD_ORDERS = ("zxyc", "zyxc", "zyxc")
FORWARD_SLOTS = ((2, 10, 25), (2, 10, 26), (3, 11, 26))


def front_kernel(
    far_count,
    states_ref,
    states_any,
    attention_ref,
    inner_ref,
    outer_ref,
    lengths_ref,
    mixed_ref,
    qx_ref,
    extra_ref,
    weights_out,
    queries_out,
    keys_out,
    values_out,
    twin_out,
    inner_full,
    outer_full,
    wo_full,
    full,
    queries,
    keys,
    values,
    twin_states,
    twin_queries,
    inner_low,
    outer_low,
    wo_low,
    ka,
    va,
    score_a,
    score_b,
    send_sems,
    recv_sems,
    local_sems,
):
    rows = states_ref.shape[0]
    step = pl.program_id(0)
    here = Place(far_count)
    wires = Wires(send_sems, recv_sems)
    shard = full.shape[-2], full.shape[-1] // 4
    projections = [
        Gather(wires, here, full.at[member], PROJECT_ORDERS[member], whole_chunk(*shard)) for member in range(2)
    ]
    projections += [
        Gather(wires, here, full.at[2], PROJECT_ORDERS[core], whole_chunk(*shard), active=here.core == core)
        for core in range(2)
    ]
    fulls, lows = (inner_full, outer_full, wo_full), (inner_low, outer_low, wo_low)
    gathers = [
        Gather(wires, here, target, order, whole_chunk(*low.shape))
        for target, low, order in zip(fulls, lows, FORWARD_ORDERS)
    ]
    fill = [
        pltpu.make_async_copy(low, gather.home, local_sems.at[number])
        for number, (low, gather) in enumerate(zip(lows, gathers))
    ]
    swap_states = wires.copy(states_any, twin_states, here.to_twin)
    swaps = []
    for number, block in enumerate((here.model, here.beside)):
        cols = columns(block, PAIR)
        for kept in (keys, values):
            for start, end in ((0, rows), (rows, 0)):
                swaps.append(
                    wires.copy(kept.at[pl.ds(start, rows), cols], kept.at[pl.ds(end, rows), cols], here.to_twin)
                )
        swaps.append(wires.copy(twin_queries.at[number], queries.at[:, cols], here.to_twin))
    outward = [
        pltpu.make_async_copy(source, target, local_sems.at[3 + number])
        for number, (source, target) in enumerate(
            ((queries, queries_out), (keys, keys_out), (values, values_out), (twin_states, twin_out), (full, weights_out))
        )
    ]

    @pl.when(step == 0)
    def _():
        for member in range(3):
            full[member, here.far, here.near, :, columns(here.model, shard[1])] = attention_ref[member].astype(BF16)
        inner_low[...] = inner_ref[...].astype(BF16)
        outer_low[...] = outer_ref[...].astype(BF16)
        wo_low[...] = attention_ref[3].astype(BF16)
        start_all(fill)
        here.meet()
        for gather in projections:
            gather.begin()
        swap_states.start()
        index = lax.broadcasted_iota(jnp.int32, (2 * rows, 1), 0)
        half = here.model % 2
        position = jnp.where(index < rows, index + half * rows, index - half * rows)
        bias = jnp.where(position < lengths_ref[here.side], 0.0, -1e30)
        lane = lane_in_half()
        extra_ref[...] = jnp.where(lane == 0, bias, jnp.where(lane <= 3, 1.0, 0.0)).astype(BF16)
        wait_all(fill)
        for gather in projections:
            gather.advance(0)
        for gather in gathers:
            gather.begin()
        for gather in projections:
            gather.advance(1)
        swap_states.wait()
        for gather in projections:
            gather.advance(2)
        for member, kept in ((1, keys), (2, values), (0, queries)):
            both = jnp.concatenate(
                [full[member, :, :, :, columns(block, PAIR)].reshape(D, PAIR) for block in (here.model, here.beside)],
                axis=1,
            )
            own = mm(states_ref[...], both).astype(BF16)
            twin = mm(twin_states[...], both).astype(BF16)
            if member == 0:
                own = (own * DH ** (-0.5)).astype(BF16)
                twin = (twin * DH ** (-0.5)).astype(BF16)
            for number, block in enumerate((here.model, here.beside)):
                cols = columns(block, PAIR)
                kept[:rows, cols] = own[:, number * PAIR : (number + 1) * PAIR]
                if member:
                    kept[rows:, cols] = twin[:, number * PAIR : (number + 1) * PAIR]
                else:
                    twin_queries[number] = twin[:, number * PAIR : (number + 1) * PAIR]
        start_all(swaps)

    @pl.when(step == 2)
    def _():
        wait_all(swaps)
        for gather in projections:
            gather.advance(3)
        start_all(outward)

    calls = [
        (slot, functools.partial(gather.advance, number))
        for gather, slots in zip(gathers, FORWARD_SLOTS)
        for number, slot in enumerate(slots)
    ]
    at = slot_calls(step, 2 * (rows // QUERY_ROWS), calls)
    pair_cols = columns(2 * (step % 2) + (step // 2 + here.core) % 2, PAIR)
    place = lane_in_half()
    first = jnp.where(place == 0, 1.0, 0.0).astype(BF16)
    ones = jnp.where(place <= 3, 1.0, 0.0).astype(BF16)
    for parity in range(2):
        ka[parity] = blend(parity, keys[:, pair_cols], extra_ref[...])
        va[parity] = blend(parity, values[:, pair_cols], ones)
    steps = [(parity, block) for block in range(rows // QUERY_ROWS) for parity in range(2)]
    scratch = (score_a, score_b)

    chunk = keys.shape[0] // FORWARD_CHUNKS

    def query_part(index):
        parity, block = steps[index]
        return blend(parity, queries[pl.ds(block * QUERY_ROWS, QUERY_ROWS), pair_cols], first)

    def score(index, part, number):
        window = pl.ds(number * chunk, chunk)
        scores = mm(ka[steps[index][0], window, :], part, NT)
        scratch[index % 2][window, :] = scores
        return jnp.max(scores, axis=0, keepdims=True)

    part = query_part(0)
    row_max = score(0, part, 0)
    for number in range(1, FORWARD_CHUNKS):
        row_max = jnp.maximum(row_max, score(0, part, number))
    held = [None, None]
    logs = [None, None]
    row = lax.broadcasted_iota(jnp.int32, (PAIR, 1), 0)
    for index, (parity, block) in enumerate(steps):
        at(index)
        more = index + 1 < len(steps)
        part = query_part(index + 1) if more else None
        product, next_max = None, None
        for number in range(FORWARD_CHUNKS):
            if more:
                found = score(index + 1, part, number)
                next_max = found if number == 0 else jnp.maximum(next_max, found)
            window = pl.ds(number * chunk, chunk)
            shifted = jnp.exp(scratch[index % 2][window, :] - row_max).astype(BF16)
            term = mm(va[parity, window, :], shifted, TN)
            product = term if number == 0 else product + term
        sum_row = DH if parity == 0 else 0
        total = product[sum_row : sum_row + 1, :]
        held[parity] = product / total
        logs[parity] = row_max + jnp.log(total)
        row_max = next_max
        if parity == 1:
            window = pl.ds(block * QUERY_ROWS, QUERY_ROWS)
            both = jnp.concatenate([held[0][:DH], held[1][DH:]], axis=0)
            mixed_ref[window, pair_cols] = both.T
            parts = split3(-jnp.where(row < DH, logs[1], logs[0]))
            spot = row % DH
            extra = jnp.where(spot == 0, 1.0, 0.0)
            for number, part in enumerate(parts):
                extra = jnp.where(spot == number + 1, part, extra)
            qx_ref[window, pair_cols] = extra.T.astype(BF16)

    @pl.when(step == pl.num_programs(0) - 1)
    def _():
        for gather in gathers:
            gather.advance(GATHER_STEPS - 1)
        wait_all(outward)


def once(shape):
    return pl.BlockSpec(shape, lambda j: (0,) * len(shape), pipeline_mode=pl.Buffered(1))


def front(states, attention_weights, inner_shard, outer_shard, lengths, far_count):
    rows, width = states.shape
    total = 2 * rows
    shard_rows = attention_weights.shape[1]
    fulls = [
        jax.ShapeDtypeStruct((far_count, 2, height, wide), BF16)
        for height, wide in ((inner_shard.shape[0], FF), (outer_shard.shape[0], D), (shard_rows, D))
    ]
    copies = 7 * gather_copies(far_count) + 11
    weights_shape = (3, far_count, 2, shard_rows, D)
    return pl.pallas_call(
        functools.partial(front_kernel, far_count),
        name="front",
        grid=(width // PAIR,),
        in_specs=[once(states.shape), any_spec()]
        + [once(item.shape) for item in (attention_weights, inner_shard, outer_shard)]
        + [smem_spec()],
        out_specs=[once((rows, width)), once((rows, width)), once((total, PAIR))] + [any_spec()] * 8,
        out_shape=[
            jax.ShapeDtypeStruct((rows, width), F32),
            jax.ShapeDtypeStruct((rows, width), BF16),
            jax.ShapeDtypeStruct((total, PAIR), BF16),
            jax.ShapeDtypeStruct(weights_shape, BF16),
            jax.ShapeDtypeStruct((rows, width), BF16),
            jax.ShapeDtypeStruct((total, width), BF16),
            jax.ShapeDtypeStruct((total, width), BF16),
            jax.ShapeDtypeStruct((rows, width), BF16),
        ]
        + fulls,
        scratch_shapes=[
            pltpu.VMEM(weights_shape, BF16),
            pltpu.VMEM((rows, width), BF16),
            pltpu.VMEM((total, width), BF16),
            pltpu.VMEM((total, width), BF16),
            pltpu.VMEM((rows, width), BF16),
            pltpu.VMEM((2, rows, PAIR), BF16),
            pltpu.VMEM(inner_shard.shape, BF16),
            pltpu.VMEM(outer_shard.shape, BF16),
            pltpu.VMEM(attention_weights.shape[1:], BF16),
            pltpu.VMEM((2, total, PAIR), BF16),
            pltpu.VMEM((2, total, PAIR), BF16),
            pltpu.VMEM((total, QUERY_ROWS), F32),
            pltpu.VMEM((total, QUERY_ROWS), F32),
            pltpu.SemaphoreType.DMA((copies,)),
            pltpu.SemaphoreType.DMA((copies,)),
            pltpu.SemaphoreType.DMA((8,)),
        ],
        compiler_params=pltpu.CompilerParams(
            vmem_limit_bytes=VMEM_LIMIT, collective_id=1, has_side_effects=True
        ),
    )(states, states, attention_weights, inner_shard, outer_shard, lengths)


EARLY = (
    (0, 0, "yxz", "zyxc"),
    (1, 0, "xyz", "zxyc"),
    (2, None, "xyz", "zxyc"),
    (0, 1, "yxz", "zyxc"),
    (1, 1, "xyz", "zxyc"),
)
LATE_REDUCE = ("yxz", "xyz", "yxz")
LATE_GATHER = ("zyxc", "zxyc", "zyxc")
SCHEDULE = (
    (0, 0, 0), (0, 1, 0), (5, 0, 1), (5, 1, 1), (11, 0, 2), (11, 1, 2),
    (11, 2, 0), (11, 3, 0), (11, 4, 0), (15, 2, 1), (16, 0, 3), (16, 1, 3),
    (16, 3, 1), (16, 4, 1), (18, 2, 2), (19, 5, 1), (19, 6, 1), (19, 7, 1),
    (21, 0, 4), (21, 1, 4), (23, 2, 3), (23, 4, 2), (23, 6, 2), (24, 3, 2),
    (24, 5, 2), (24, 7, 2), (26, 0, 5), (26, 1, 5), (26, 2, 4), (26, 6, 3),
    (27, 4, 3), (28, 5, 3), (28, 7, 3), (29, 6, 4), (30, 1, 6), (30, 2, 5),
    (30, 3, 3), (31, 0, 6), (31, 5, 4), (31, 7, 4), (32, 6, 5), (32, 4, 4),
    (32, 2, 6), (32, -1, 0), (32, -1, 1), (32, 5, 5), (32, 7, 5), (32, 3, 4),
    (32, 10, 1), (32, 8, 1), (32, 9, 1), (32, 6, 6), (32, 1, 7), (32, 4, 5),
    (32, 0, 7), (32, 5, 6), (32, 7, 6), (32, 3, 5), (32, 1, 8), (32, 2, 7),
    (32, 10, 2), (32, 8, 2), (32, 0, 8), (32, 6, 7), (32, 9, 2), (32, 2, 8),
    (32, 6, 8), (32, 10, 3), (32, 8, 3), (32, 5, 7), (32, 7, 7), (32, 3, 6),
    (32, 4, 6), (32, 9, 3), (32, 10, 4), (32, 8, 4), (32, 5, 8), (32, 7, 8),
    (32, 9, 4), (32, -1, 11), (32, 10, 5), (32, 8, 5), (32, -1, 12), (32, 9, 5),
    (32, 3, 7), (32, 4, 7), (32, -1, 13), (32, 10, 6), (32, 8, 6), (32, 9, 6),
    (32, -1, 14), (32, 3, 8), (32, 4, 8), (32, -1, 2), (32, -1, 3), (32, -1, 4),
    (32, 10, 7), (32, 8, 7), (32, 9, 7), (32, -1, 15), (32, -1, 5), (32, -1, 6),
    (32, -1, 7), (32, -1, 8), (32, -1, 9), (32, 10, 8), (32, 8, 8), (32, 9, 8),
    (32, -1, 10),
)
NORM_SLOTS = (4, 7, 12, 16)


def early_chunks(shapes):
    chunks = []
    for array, half, *_ in EARLY:
        rows, cols = shapes[array]
        if half is None:
            chunks.append(whole_chunk(rows, cols))
        elif array == 0:
            chunks.append(Chunk((0, rows), (half * cols // 2, cols // 2), rows, cols))
        else:
            chunks.append(Chunk((half * rows // 2, rows // 2), (0, cols), rows, cols))
    return chunks


def product_steps(grad, left_root, right_root, place, counts, left_out, right_out, update_out, room, held):
    data_count, model_count = counts
    far_count, _, shard_rows, width = grad.shape
    height = data_count * shard_rows
    part = far_count // model_count
    size = width // model_count
    share = width // data_count

    def left():
        rows_here = grad[place.far, place.near]
        rows_there = grad[pl.ds(place.model * part, part)].reshape(height // model_count, width)
        left_out[...] = mm(rows_here, rows_there, NT)

    def right():
        cols_there = grad[:, :, :, columns(place.model, size)].reshape(height, size)
        if share % 128 == 0:
            cols_here = grad[:, :, :, columns(place.data_rank, share)].reshape(height, share)
            right_out[...] = mm(cols_here, cols_there, TN)
        else:
            group = data_count // model_count
            cols_here = grad[:, :, :, columns(place.data_rank // group, size)].reshape(height, size)
            room[:size, :size] = mm(cols_here, cols_there, TN)
            window = pl.ds(pl.multiple_of((place.data_rank % group) * share, share), share)
            right_out[...] = room[window, :size]

    def once():
        whole = grad[...].reshape(height, width)
        high, low = split2(left_root[...])
        held[...] = mm(high, whole) + mm(low, whole)

    def twice():
        chunk = min(512, width)
        total = jnp.zeros(update_out.shape, F32)
        for start in range(0, width, chunk):
            high, low = split2(held[:, start : start + chunk])
            root_high, root_low = split2(right_root[start : start + chunk, :])
            total = total + (mm(high, root_high) + mm(high, root_low) + mm(low, root_high))
        update_out[...] = total

    return [left, right, once, twice]


def backward_kernel(
    far_count,
    counts,
    inv_tokens,
    q_ref,
    qx_ref,
    k_ref,
    v_ref,
    kx_ref,
    do_ref,
    dox_ref,
    own_any_states,
    twin_any_states,
    weights_any,
    norm_raw,
    skip_any,
    inner_low,
    outer_low,
    wo_low,
    *rest,
):
    roots_any, rest = rest[:6], rest[6:]
    (inner_piece, outer_piece, wo_piece, norm_total, late_out, squares_out, own_any, twin_in), rest = rest[:8], rest[8:]
    products, rest = rest[:9], rest[9:]
    (qa, da, ka, va, dqt, dq, dk, dv, states_t, late_low, own_sum, twin_out), rest = rest[:12], rest[12:]
    mine, rest = rest[: len(EARLY)], rest[len(EARLY) :]
    count = len(EARLY) * REDUCE_BUFFERS
    early_buffers, rest = rest[:count], rest[count:]
    late_buffers, rest = rest[: 3 * REDUCE_BUFFERS], rest[3 * REDUCE_BUFFERS :]
    roots, rest = rest[:6], rest[6:]
    (own_states, twin_states, weights_ref), rest = rest[:3], rest[3:]
    (attention_full, inner_full, outer_full, room, held_small, held_wide, held_tall), rest = rest[:7], rest[7:]
    tile, tile_stages, tile_slots, norm_tile, norm_stages, norm_slots = rest[:6]
    send_sems, recv_sems, load_sems, local_sems = rest[6:]

    step = pl.program_id(0)
    rows = q_ref.shape[0]
    total = k_ref.shape[0]
    place = Place(far_count)
    wires = Wires(send_sems, recv_sems)
    lows = (inner_low, outer_low, wo_low)
    pieces = (inner_piece, outer_piece, wo_piece)
    fulls = (inner_full, outer_full, attention_full.at[3])
    chunks = early_chunks([piece.shape for piece in pieces])
    reducers = []
    gathers = []
    loads = []
    for number, (array, _, reduce_order, gather_order) in enumerate(EARLY):
        buffers = early_buffers[number * REDUCE_BUFFERS : (number + 1) * REDUCE_BUFFERS]
        reducer = Reducer(wires, place, buffers, reduce_order, low=lows[array], chunk=chunks[number])
        reducers.append(reducer)
        loads.append(reducer.loads(lows[array], mine[number], load_sems.at[number]))
        gathers.append(Gather(wires, place, fulls[array], gather_order, chunks[number]))
    late_shape = wo_piece.shape
    late_reducers = []
    late_gathers = []
    for late_set in range(2):
        active = place.core == late_set
        late_reducers.append(
            [
                Reducer(
                    wires,
                    place,
                    late_buffers[member * REDUCE_BUFFERS : (member + 1) * REDUCE_BUFFERS],
                    LATE_REDUCE[member],
                    given=late_low.at[member],
                    active=active,
                )
                for member in range(3)
            ]
        )
        late_gathers.append(
            [
                Gather(
                    wires, place, attention_full.at[member], LATE_GATHER[member], whole_chunk(*late_shape), active=active
                )
                for member in range(3)
            ]
        )
    norms = Spread(wires, place, norm_tile, norm_stages, norm_slots)
    squares = Spread(wires, place, tile, tile_stages, tile_slots)
    swap = wires.copy(twin_out, twin_in, place.to_twin)
    fetch = [
        pltpu.make_async_copy(source, target, local_sems.at[number])
        for number, (source, target) in enumerate(
            zip((*roots_any, skip_any, weights_any), (*roots, own_sum, weights_ref))
        )
    ]
    outward = pltpu.make_async_copy(own_sum, own_any, local_sems.at[0])
    bring = [
        pltpu.make_async_copy(own_any_states, own_states, local_sems.at[8]),
        pltpu.make_async_copy(twin_any_states, twin_states, local_sems.at[9]),
    ]

    def turn_states():
        wait_all(bring)
        states_t[:, :rows] = own_states[...].T
        states_t[:, rows:] = twin_states[...].T


    def early_call(number, number_of_step):
        array, chunk = EARLY[number][0], chunks[number]
        if number_of_step == 0:

            def call():
                reducers[number].begin()
                start_all(loads[number])

        elif number_of_step <= REDUCE_STEPS:

            def call():
                if number_of_step == 1:
                    wait_all(loads[number])
                reducers[number].advance(number_of_step - 1)
                if number_of_step == REDUCE_STEPS:
                    piece = reducers[number].result() * inv_tokens
                    pieces[array][chunk.row_window, pl.ds(*chunk.cols)] = piece
                    gathers[number].home[...] = piece.astype(BF16)
                    gathers[number].begin()

        else:

            def call():
                gathers[number].advance(number_of_step - REDUCE_STEPS - 1)

        return call

    def late_products():
        slot = (step + place.side) % 2
        wide = jnp.concatenate([dk[:, pair_cols], dv[:, pair_cols]], axis=1)
        both = mm(states_t[...], wide)
        values = (mm(states_t[:, :rows], dq[:, pair_cols]), both[:, :PAIR], both[:, PAIR:])
        active = place.core == step // 2
        for member, value in enumerate(values):
            parts = value.reshape(far_count, 2, *late_shape)

            @pl.when(active)
            def _():
                for near in range(2):
                    late_reducers[0][member].acc[slot, near] = parts[:, near]

            @pl.when(jnp.logical_not(active))
            def _():
                for near in range(2):
                    late_low[member, slot, near] = parts[:, near].astype(BF16)

    def late_call(late_set, member, number_of_step):
        reducer, gather = late_reducers[late_set][member], late_gathers[late_set][member]
        if number_of_step == 0:
            return reducer.begin

        def call():
            if number_of_step <= REDUCE_STEPS:
                reducer.advance(number_of_step - 1)
                if number_of_step == REDUCE_STEPS:

                    @pl.when(place.core == late_set)
                    def _():
                        piece = reducer.result() * inv_tokens
                        late_out[member] = piece
                        gather.home[...] = piece.astype(BF16)

                    gather.begin()
            else:
                gather.advance(number_of_step - REDUCE_STEPS - 1)

        return call

    def scheduled(chain, number_of_step):
        if chain < len(EARLY):
            return early_call(chain, number_of_step)
        return late_call(*divmod(chain - len(EARLY), 3), number_of_step)

    sub_steps = 4 * (total // KEY_ROWS)
    calls = [(slot, scheduled(chain, number)) for slot, chain, number in SCHEDULE if slot < sub_steps]
    calls += [(slot, functools.partial(norms.advance, stage)) for stage, slot in enumerate(NORM_SLOTS)]
    calls.append((12, lambda: start_all(fetch)))
    calls.append((6, turn_states))
    at = slot_calls(step, total // KEY_ROWS, calls)

    @pl.when(step == 0)
    def _():
        norm_tile[...] = norm_raw[...]
        place.meet()
        norms.begin()
        start_all(bring)

    lane = lane_in_half()
    ones = jnp.where(lane <= 3, 1.0, 0.0).astype(BF16)
    for parity in range(2):
        ka[parity] = blend(parity, k_ref[...], kx_ref[...])
        va[parity] = blend(parity, v_ref[...], ones)
        qa[parity] = blend(parity, q_ref[...], qx_ref[...])
        da[parity] = blend(parity, do_ref[...], dox_ref[...])
    dqt[...] = jnp.zeros_like(dqt)
    pair = 2 * (step % 2) + step // 2
    pair_cols = columns(pair, PAIR)
    for block in range(total // KEY_ROWS):
        at(block)
        window = pl.ds(block * KEY_ROWS, KEY_ROWS)
        key_grads = []
        value_grads = []
        for parity in range(2):
            key_block = ka[parity, window, :]
            probs = jnp.exp(mm(key_block, qa[parity], NT))
            d_probs = mm(va[parity, window, :], da[parity], NT)
            d_scores = (probs * d_probs).astype(BF16)
            value_grads.append(mm(probs.astype(BF16), da[parity]))
            key_grads.append(mm(d_scores, qa[parity]))
            dqt[parity] += mm(key_block, d_scores, TN)
        dk[window, pair_cols] = jnp.where(own_lanes(0), key_grads[0], key_grads[1]).astype(BF16)
        dv[window, pair_cols] = jnp.where(own_lanes(0), value_grads[0], value_grads[1]).astype(BF16)
    both = jnp.concatenate([dqt[0, :DH], dqt[1, DH:]], axis=0) * DH ** (-0.5)
    dq[:, pair_cols] = both.T.astype(BF16)

    late_products()
    for late_set in range(2):

        @pl.when(step == 2 * late_set + 1)
        def _():
            for member in range(3):
                late_call(late_set, member, 0)()

    @pl.when(step == pl.num_programs(0) - 1)
    def _():
        part = 256

        def twin_share():
            wait_all(fetch)

            @pl.loop(0, rows // part)
            def _(block):
                window = pl.ds(pl.multiple_of(block * part, part), part)
                there = pl.ds(pl.multiple_of(rows + block * part, part), part)
                value = mm(dk[there, :], weights_ref[1], NT) + mm(dv[there, :], weights_ref[2], NT)
                twin_out[window, :] = value.astype(BF16)

            swap.start()

        def own_share():
            @pl.loop(0, rows // part)
            def _(block):
                window = pl.ds(pl.multiple_of(block * part, part), part)
                own_sum[window, :] += (
                    mm(dq[window, :], weights_ref[0], NT)
                    + mm(dk[window, :], weights_ref[1], NT)
                    + mm(dv[window, :], weights_ref[2], NT)
                )

            outward.start()

        common = (place, counts)
        inner_steps = product_steps(inner_full, roots[2], roots[3], *common, *products[3:6], room, held_wide)
        outer_steps = product_steps(outer_full, roots[4], roots[5], *common, *products[6:9], room, held_tall)

        def member_products():
            @pl.loop(0, 4)
            def _(member):
                steps = product_steps(
                    attention_full.at[member],
                    roots[0].at[member],
                    roots[1].at[member],
                    *common,
                    *[product.at[member] for product in products[:3]],
                    room,
                    held_small,
                )
                for call in steps:
                    call()

        work = [twin_share, own_share, *outer_steps, *inner_steps, member_products]

        def square(piece):
            return jnp.sum(jnp.sum(piece * piece, axis=0, keepdims=True), axis=1, keepdims=True)

        def squares_begin():
            square_sum = square(inner_piece[...]) + square(outer_piece[...]) + square(wo_piece[...])
            for member in range(3):
                square_sum = square_sum + square(late_out[member])
            tile[...] = jnp.broadcast_to(square_sum, tile.shape)
            squares.begin()

        work.append(squares_begin)
        work += [functools.partial(squares.advance, stage) for stage in range(4)]
        for slot, chain, number in SCHEDULE:
            if slot >= sub_steps:
                (work[number] if chain < 0 else scheduled(chain, number))()
        squares_out[...] = tile[...]
        norm_total[...] = norm_tile[...] * inv_tokens
        swap.wait()
        outward.wait()


def backward(
    queries,
    query_extra,
    keys,
    values,
    key_extra,
    d_mixed,
    d_extra,
    states,
    twin_states,
    weights,
    norm_rows,
    skip,
    lows,
    roots,
    counts,
):
    rows, width = queries.shape
    total = keys.shape[0]
    data_count, model_count = counts
    far_count = data_count // 2

    def by_pair(height):
        return pl.BlockSpec((height, PAIR), lambda j: (0, 2 * (j % 2) + j // 2))

    whole = once

    def seen(array):
        return array.reshape(far_count, 2, array.shape[0] // data_count, array.shape[1])

    def products(lead, height, wide):
        return [
            jax.ShapeDtypeStruct(lead + shape, F32)
            for shape in (
                (height // data_count, height // model_count),
                (wide // data_count, wide // model_count),
                (height // data_count, wide // model_count),
            )
        ]

    pieces = [(low.shape[0] // data_count, low.shape[1] // model_count) for low in lows]
    late = pieces[2]
    tile = (8, 128)
    out_shape = [jax.ShapeDtypeStruct(piece, F32) for piece in pieces]
    out_shape += [
        jax.ShapeDtypeStruct(norm_rows.shape, F32),
        jax.ShapeDtypeStruct((3,) + late, F32),
        jax.ShapeDtypeStruct(tile, F32),
        jax.ShapeDtypeStruct((rows, width), F32),
        jax.ShapeDtypeStruct((rows, width), BF16),
    ]
    out_specs = [whole(item.shape) for item in out_shape[:6]] + [any_spec()] * 2
    tail = products((4,), D, D) + products((), D, FF) + products((), FF, D)
    out_shape += tail
    out_specs += [whole(item.shape) for item in tail]
    shard_rows = D // data_count
    scratch = [
        pltpu.VMEM((2, rows, PAIR), BF16),
        pltpu.VMEM((2, rows, PAIR), BF16),
        pltpu.VMEM((2, total, PAIR), BF16),
        pltpu.VMEM((2, total, PAIR), BF16),
        pltpu.VMEM((2, PAIR, rows), F32),
        pltpu.VMEM((rows, width), BF16),
        pltpu.VMEM((total, width), BF16),
        pltpu.VMEM((total, width), BF16),
        pltpu.VMEM((width, total), BF16),
        pltpu.VMEM((3, 2, 2, far_count) + late, BF16),
        pltpu.VMEM((rows, width), F32),
        pltpu.VMEM((rows, width), BF16),
    ]
    scratch += [pltpu.VMEM((2, 2, far_count) + chunk.shape, BF16) for chunk in early_chunks(pieces)]
    for (_, _, order, _), chunk in zip(EARLY, early_chunks(pieces)):
        scratch += reduce_scratch(order, far_count, *chunk.shape)
    for member in range(3):
        scratch += reduce_scratch(LATE_REDUCE[member], far_count, *late)
    scratch += [pltpu.VMEM(root.shape, F32) for root in roots]
    scratch += [pltpu.VMEM(item.shape, BF16) for item in (states, twin_states, weights)]
    scratch += [
        pltpu.VMEM((4, far_count, 2, shard_rows, D), BF16),
        pltpu.VMEM((far_count, 2, shard_rows, FF), BF16),
        pltpu.VMEM((far_count, 2, FF // data_count, D), BF16),
        pltpu.VMEM((FF // model_count, FF // model_count), F32),
        pltpu.VMEM((shard_rows, D), F32),
        pltpu.VMEM((shard_rows, FF), F32),
        pltpu.VMEM((FF // data_count, D), F32),
    ]
    scratch += spread_scratch(far_count, tile) + spread_scratch(far_count, norm_rows.shape)
    chains = len(EARLY) + 6
    copies = chains * (reduce_copies(far_count) + gather_copies(far_count)) + 2 * spread_copies(far_count) + 1
    scratch += [
        pltpu.SemaphoreType.DMA((copies,)),
        pltpu.SemaphoreType.DMA((copies,)),
        pltpu.SemaphoreType.DMA((len(EARLY), 4)),
        pltpu.SemaphoreType.DMA((10,)),
    ]
    return pl.pallas_call(
        functools.partial(backward_kernel, far_count, counts, 1.0 / (rows * data_count * model_count)),
        name="backward",
        grid=(width // PAIR,),
        in_specs=[by_pair(rows), by_pair(rows), by_pair(total), by_pair(total), whole((total, PAIR))]
        + [by_pair(rows), by_pair(rows)]
        + [any_spec()] * 3
        + [whole(norm_rows.shape)]
        + [any_spec()] * 10,
        out_specs=out_specs,
        out_shape=out_shape,
        scratch_shapes=scratch,
        compiler_params=pltpu.CompilerParams(
            vmem_limit_bytes=BACKWARD_VMEM, collective_id=2, has_side_effects=True
        ),
    )(
        queries,
        query_extra,
        keys,
        values,
        key_extra,
        d_mixed,
        d_extra,
        states,
        twin_states,
        weights,
        norm_rows,
        skip,
        *[seen(low) for low in lows],
        *roots,
    )


def finish_kernel(limit, rate, squares_ref, norm_ref, own_ref, twin_ref, late_ref, *rest):
    (inner_piece, outer_piece, wo_piece, gains_ref, biases_ref), rest = rest[:5], rest[5:]
    stats, rest = rest[:6], rest[6:]
    products, rest = rest[:6], rest[6:]
    weights, rest = rest[:3], rest[3:]
    updates, rest = rest[:3], rest[3:]
    (states_out, norm_out, attention_grad, inner_grad, outer_grad, norm_grad), rest = rest[:6], rest[6:]
    weights_new, norm_new, stats_new = rest[:3], rest[3], rest[4:]
    norms = norm_ref[0:4, :]
    norm_square = jnp.sum(jnp.sum(norms * norms, axis=0, keepdims=True), axis=1, keepdims=True)
    grad_norm = jnp.sqrt(squares_ref[0:1, 0:1] + norm_square)
    norm_out[...] = grad_norm
    factor = jnp.minimum(1.0, limit / grad_norm)
    states_out[...] = (own_ref[...] + twin_ref[...].astype(F32)).astype(BF16)
    for member in range(3):
        attention_grad[member] = late_ref[member] * factor
    attention_grad[3] = wo_piece[...] * factor
    inner_grad[...] = inner_piece[...] * factor
    outer_grad[...] = outer_piece[...] * factor
    share = norm_grad.shape[-1]
    start = (lax.axis_index("dp") * lax.axis_size("mp") + lax.axis_index("mp")) * share
    params = jnp.concatenate([gains_ref[...], biases_ref[...]], axis=0)
    row = lax.broadcasted_iota(jnp.int32, (4, 1), 0) == start // D

    def share_of(table):
        picked = jnp.sum(jnp.where(row, table, 0.0), axis=0, keepdims=True)
        return pltpu.roll(jnp.broadcast_to(picked, (8, D)), (D - start % D) % D, 1)[0:1, :share]

    clipped = share_of(norms) * factor
    norm_grad[...] = clipped
    norm_new[...] = share_of(params) - rate * clipped
    for weight, change, out in zip(weights, updates, weights_new):
        out[...] = weight[...] - (step_rate * factor) * change[...]
    for stat, product, out in zip(stats, products, stats_new):
        out[...] = 0.5 * stat[...] + (0.5 * factor * factor) * product[...]


def finish(token_total, norm_share, squares, norm_rows, own, twin, late, pieces, gains, biases, stats, products, weights, updates):
    limit = 0.01 * math.sqrt((4 * D * D + 2 * D * FF + 4 * D) / token_total)
    rate = 20.0 * math.sqrt(token_total)
    inner_piece, outer_piece, _ = pieces
    shapes = [
        jax.ShapeDtypeStruct(own.shape, BF16),
        jax.ShapeDtypeStruct((1, 1), F32),
        jax.ShapeDtypeStruct(weights[0].shape, F32),
        jax.ShapeDtypeStruct(inner_piece.shape, F32),
        jax.ShapeDtypeStruct(outer_piece.shape, F32),
        jax.ShapeDtypeStruct((1, norm_share), F32),
    ]
    shapes += [jax.ShapeDtypeStruct(weight.shape, F32) for weight in weights]
    shapes.append(jax.ShapeDtypeStruct((1, norm_share), F32))
    shapes += [jax.ShapeDtypeStruct(stat.shape, F32) for stat in stats]
    operands = (squares, norm_rows, own, twin, late, *pieces, gains, biases)
    operands += (*stats, *products, *weights, *updates)
    return pl.pallas_call(
        functools.partial(finish_kernel, limit, rate),
        name="finish",
        in_specs=[vmem_spec()] * len(operands),
        out_specs=[vmem_spec()] * len(shapes),
        out_shape=shapes,
        compiler_params=pltpu.CompilerParams(vmem_limit_bytes=VMEM_LIMIT),
    )(*operands)


def middle_kernel(
    mixed_ref,
    states_ref,
    cotangent_ref,
    halting_ref,
    wo_ref,
    inner_any,
    outer_any,
    gains_ref,
    biases_ref,
    out_ref,
    dm_ref,
    dx_ref,
    skip_ref,
    norm_raw,
    inner_out,
    outer_out,
    wo_low,
    inner_ref,
    outer_ref,
    inner_low,
    outer_low,
    sems,
    gelu_slope,
    activated_ref,
    d_inner_ref,
    normed_ref,
    branch_ref,
    attended_ref,
    mixed_low_ref,
):
    step = pl.program_id(0)
    bring = [
        pltpu.make_async_copy(inner_any, inner_ref, sems.at[0]),
        pltpu.make_async_copy(outer_any, outer_ref, sems.at[1]),
    ]
    pl.when(step == 0)(lambda: start_all(bring))
    tokens = pl.ds(pl.multiple_of(step * TOKEN_ROWS, TOKEN_ROWS), TOKEN_ROWS)
    head_row = lax.broadcasted_iota(jnp.int32, (D, D), 0) // DH
    head_col = lax.broadcasted_iota(jnp.int32, (D, D), 1) // DH
    swap = jnp.where(head_row + 1 - 2 * (head_row % 2) == head_col, 1.0, 0.0).astype(BF16)

    def mean(value):
        return jnp.mean(value, axis=-1, keepdims=True)

    def total(value):
        return jnp.sum(value, axis=0, keepdims=True)

    def normalize(residual):
        centered = residual - mean(residual)
        scale = lax.rsqrt(mean(centered * centered) + epsilon)
        return centered * scale, scale

    def norm_back(d_out, gain, unit, scale):
        d_unit = d_out * gain
        return (d_unit - mean(d_unit) - unit * mean(d_unit * unit)) * scale

    mixed = mixed_ref[...]
    mixed_low = mixed.astype(BF16)
    hidden = states_ref[...].astype(F32)
    upstream = cotangent_ref[...].astype(F32)
    table = halting_ref[...].astype(F32).T
    lane = lax.broadcasted_iota(jnp.int32, (1, table.shape[1]), 1)
    here = step * (TOKEN_ROWS // 128)
    flags = [
        jnp.sum(jnp.where(lane == here + row, table, 0.0), axis=1, keepdims=True) for row in range(TOKEN_ROWS // 128)
    ]
    running = jnp.concatenate(flags, axis=0) == 1.0
    gain1, gain2 = gains_ref[0:1, :], gains_ref[1:2, :]
    unit1, scale1 = normalize(hidden + mm(mixed_low, wo_ref[...]))
    normed = unit1 * gain1 + biases_ref[0:1, :]
    normed_low = normed.astype(BF16)
    rate = math.sqrt(2.0 / math.pi)
    parts = [pl.ds(start, FF_PART) for start in range(0, FF, FF_PART)]
    branch = None
    pl.when(step == 0)(lambda: wait_all(bring))
    inner = mm(normed_low, inner_ref[:, parts[0]])
    for number, part in enumerate(parts):
        ahead = mm(normed_low, inner_ref[:, parts[number + 1]]) if number + 1 < len(parts) else None
        square = inner * inner
        bend = jnp.tanh(rate * inner * (1.0 + 0.044715 * square))
        half = 0.5 * (1.0 + bend)
        value = (inner * half).astype(BF16)
        activated_ref[tokens, part] = value
        gelu_slope[:, part] = half + 0.5 * inner * (1.0 - bend * bend) * (rate * (1.0 + 3 * 0.044715 * square))
        term = mm(value, outer_ref[part, :])
        branch = term if number == 0 else branch + term
        inner = ahead
    unit2, scale2 = normalize(normed + branch)
    final = unit2 * gain2 + biases_ref[1:2, :]
    out_ref[...] = jnp.where(running, final, hidden).astype(BF16)
    d_final = jnp.where(running, upstream, 0.0)
    d_resid2 = norm_back(d_final, gain2, unit2, scale2)
    d_branch = d_resid2.astype(BF16)
    d_normed = d_resid2
    d_act = mm(d_branch, outer_ref[parts[0], :], NT)
    for number, part in enumerate(parts):
        ahead = mm(d_branch, outer_ref[parts[number + 1], :], NT) if number + 1 < len(parts) else None
        d_inner = (d_act * gelu_slope[:, part]).astype(BF16)
        d_inner_ref[tokens, part] = d_inner
        d_normed = d_normed + mm(d_inner, inner_ref[:, part], NT)
        d_act = ahead
    d_resid1 = norm_back(d_normed, gain1, unit1, scale1)
    d_attended = d_resid1.astype(BF16)
    normed_ref[tokens, :] = normed_low
    branch_ref[tokens, :] = d_branch
    attended_ref[tokens, :] = d_attended
    mixed_low_ref[tokens, :] = mixed_low
    d_mixed = mm(d_attended, wo_ref[...], NT).astype(BF16)
    dm_ref[...] = d_mixed
    skip_ref[...] = jnp.where(running, 0.0, upstream) + d_resid1

    @pl.when(step == 0)
    def _():
        norm_raw[...] = jnp.zeros_like(norm_raw)

    norm_raw[0:1, :] += total(d_normed * unit1)
    norm_raw[1:2, :] += total(d_final * unit2)
    norm_raw[2:3, :] += total(d_normed)
    norm_raw[3:4, :] += total(d_final)
    high, low = split2(d_mixed.astype(F32) * mixed)
    delta = mm(high, swap) + mm(low, swap)
    pieces = split3(-delta)
    place = lax.broadcasted_iota(jnp.int32, (1, D), 1) % DH
    extra = jnp.zeros_like(delta)
    for number, part in enumerate(pieces):
        extra = jnp.where(place == number + 1, part, extra)
    dx_ref[...] = extra.astype(BF16)

    @pl.when(step == pl.num_programs(0) - 1)
    def _():
        wo_low[...] = mm(mixed_low_ref[...], attended_ref[...], TN).astype(BF16)
        outward = []
        for number, part in enumerate(parts):
            outer_low[part, :] = mm(activated_ref[:, part], branch_ref[...], TN).astype(BF16)
            outward.append(
                pltpu.make_async_copy(outer_low.at[part, :], outer_out.at[part, :], sems.at[2 + 2 * number])
            )
            outward[-1].start()
            inner_low[:, part] = mm(normed_ref[...], d_inner_ref[:, part], TN).astype(BF16)
            outward.append(
                pltpu.make_async_copy(inner_low.at[:, part], inner_out.at[:, part], sems.at[3 + 2 * number])
            )
            outward[-1].start()
        wait_all(outward)


def middle(mixed, states, cotangent, halting, wo, inner, outer, gains, biases):
    rows = mixed.shape[0]
    shapes = [jax.ShapeDtypeStruct((rows, D), BF16)] * 3
    shapes += [jax.ShapeDtypeStruct((rows, D), F32), jax.ShapeDtypeStruct((8, D), F32)]
    shapes += [jax.ShapeDtypeStruct(shape, BF16) for shape in ((D, FF), (FF, D), (D, D))]
    def by_token(item):
        return pl.BlockSpec((TOKEN_ROWS, D), lambda i: (i, 0))

    operands = (mixed, states, cotangent, halting.reshape(-1, 128), wo, inner, outer, gains, biases)
    return pl.pallas_call(
        middle_kernel,
        name="middle",
        grid=(rows // TOKEN_ROWS,),
        in_specs=[by_token(item) for item in operands[:3]]
        + [once(item.shape) for item in operands[3:5]]
        + [any_spec()] * 2
        + [once(item.shape) for item in operands[7:]],
        out_specs=[by_token(item) for item in shapes[:4]]
        + [once(shapes[4].shape), any_spec(), any_spec(), once(shapes[7].shape)],
        out_shape=shapes,
        scratch_shapes=[
            pltpu.VMEM((D, FF), BF16),
            pltpu.VMEM((FF, D), BF16),
            pltpu.VMEM((D, FF), BF16),
            pltpu.VMEM((FF, D), BF16),
            pltpu.SemaphoreType.DMA((2 + 2 * (FF // FF_PART),)),
            pltpu.VMEM((TOKEN_ROWS, FF), F32),
            pltpu.VMEM((rows, FF), BF16),
            pltpu.VMEM((rows, FF), BF16),
            pltpu.VMEM((rows, D), BF16),
            pltpu.VMEM((rows, D), BF16),
            pltpu.VMEM((rows, D), BF16),
            pltpu.VMEM((rows, D), BF16),
        ],
        compiler_params=pltpu.CompilerParams(vmem_limit_bytes=VMEM_LIMIT),
    )(*operands)


def per_device(
    states,
    cotangent,
    halting,
    lengths,
    attention_weights,
    inner_weight,
    outer_weight,
    norm_gains,
    norm_biases,
    attention_left,
    attention_right,
    inner_left,
    inner_right,
    outer_left,
    outer_right,
    attention_left_root,
    attention_right_root,
    inner_left_root,
    inner_right_root,
    outer_left_root,
    outer_right_root,
):
    data_count = lax.axis_size("dp")
    model_count = lax.axis_size("mp")
    counts = (data_count, model_count)
    far_count = data_count // 2
    token_total = states.shape[0] * data_count * model_count
    (
        mixed,
        query_extra,
        key_extra,
        weights,
        queries,
        keys,
        values,
        twin_states,
        inner_full,
        outer_full,
        wo_full,
    ) = front(states, attention_weights, inner_weight, outer_weight, lengths, far_count)
    output_states, d_mixed, d_extra, skip, norm_rows, *lows = middle(
        mixed,
        states,
        cotangent,
        halting,
        wo_full.reshape(D, D),
        inner_full.reshape(D, FF),
        outer_full.reshape(FF, D),
        norm_gains,
        norm_biases,
    )
    roots = (
        attention_left_root,
        attention_right_root,
        inner_left_root,
        inner_right_root,
        outer_left_root,
        outer_right_root,
    )
    *pieces, norm_total, late, squares, own, twin, p0, p1, p2, p3, p4, p5, p6, p7, p8 = backward(
        queries,
        query_extra,
        keys,
        values,
        key_extra,
        d_mixed,
        d_extra,
        states,
        twin_states,
        weights.reshape(3, D, D),
        norm_rows,
        skip,
        lows,
        roots,
        counts,
    )
    outs = finish(
        token_total,
        4 * D // (data_count * model_count),
        squares,
        norm_total,
        own,
        twin,
        late,
        pieces,
        norm_gains,
        norm_biases,
        (attention_left, attention_right, inner_left, inner_right, outer_left, outer_right),
        (p0, p1, p3, p4, p6, p7),
        (attention_weights, inner_weight, outer_weight),
        (p2, p5, p8),
    )
    states_grad, grad_norm, attention_grad, inner_grad, outer_grad, norm_grad = outs[:6]
    attention_new, inner_new, outer_new, norm_new = outs[6:10]
    return (
        output_states,
        states_grad,
        grad_norm.reshape(()),
        attention_grad,
        inner_grad,
        outer_grad,
        norm_grad.reshape(-1),
        attention_new,
        inner_new,
        outer_new,
        norm_new.reshape(-1),
        *outs[10:],
    )


def solution(mesh):
    grid = P("dp", "mp")
    stack = P(None, "dp", "mp")
    tokens = P(("dp", "mp"), None)
    flat = P(("dp", "mp"))
    return jax.shard_map(
        per_device,
        mesh=mesh,
        in_specs=(tokens, tokens, flat, P("dp"), stack, grid, grid, P(), P())
        + (stack, stack, grid, grid, grid, grid)
        + (P(None, "dp", None), P(None, None, "mp"), P("dp", None), P(None, "mp"), P("dp", None), P(None, "mp")),
        out_specs=(tokens, tokens, P(), stack, grid, grid, flat, stack, grid, grid, flat)
        + (stack, stack, grid, grid, grid, grid),
        check_vma=False,
    )
```

profile of v0, /device:TPU:0, one launch (start us, length us, event | category | flops | bytes accessed | tf_op | source)
XLA Modules:
  0.0 200.4 jit_solution(5231542754992849856)
XLA Ops:
  0.7 52.4 %front.1 = (f32[1024,512]{1,0:T(8,128)}, bf16[1024,512]{1,0:T(8,128)(2,1)}, bf16[2048,128]{1,0:T(8,128)(2,1)}, bf16[3,4,2,64,512]{4,3,2,1,0:T(8,128)(2,1)}, bf16...) custom-call(bf16[1024,512]{1,0:T(8,128)(2,1)} %own_any_states.1, ...), custom_call_target="tpu_custom_call" | custom-call | tf_op jit(solution)/shard_map/front/pallas_call | solution.py:657
  53.0 28.8 %middle.1 = (bf16[1024,512]{1,0:T(8,128)(2,1)}, bf16[1024,512]{1,0:T(8,128)(2,1)}, bf16[1024,512]{1,0:T(8,128)(2,1)}, f32[1024,512]{1,0:T(8,128)}, f32[8,512]{1,...) custom-call(f32[1024,512]{1,0:T(8,128)} %get-tuple-element.69.mixed_ref, ...), custom_call_target="tpu_custom_call" | custom-call | tf_op jit(solution)/shard_map/middle/pallas_call | solution.py:1429
  81.9 113.1 %backward.1 = (f32[64,512]{1,0:T(8,128)}, f32[256,128]{1,0:T(8,128)}, f32[64,128]{1,0:T(8,128)}, f32[8,512]{1,0:T(8,128)}, f32[3,64,128]{2,1,0:T(8,128)}, /*inde...) custom-call(bf16[1024,512]{1,0:T(8,128)(2,1)} %get-tuple-element.74., ...), custom_call_target="tpu_custom_call" | custom-call | tf_op jit(solution)/shard_map/backward/pallas_call | solution.py:1176
  194.9 5.2 %finish.1 = (bf16[1024,512]{1,0:T(8,128)(2,1)}, f32[1,1]{1,0:T(1,128)}, f32[4,64,128]{2,1,0:T(8,128)}, f32[64,512]{1,0:T(8,128)}, f32[256,128]{1,0:T(8,128)}, /*...) custom-call(f32[8,128]{1,0:T(8,128)} %get-tuple-element.88.squares_r, ...), custom_call_target="tpu_custom_call" | custom-call | tf_op jit(solution)/shard_map/finish/pallas_call | solution.py:1263
where the time goes:
time: 199 us; the launch traced here: 200 us
  Pallas kernels  199 us (100%)
    pallas_call x1, Pallas kernels, backward(): pl.pallas_call(functools.partial(backward_kernel, far_count, counts, 1.0...  113 us
    pallas_call x1, Pallas kernels, front(): pl.pallas_call(functools.partial(front_kernel, far_count), name='front',...  52.4 us
    pallas_call x1, Pallas kernels, middle(): pl.pallas_call(middle_kernel, name='middle', grid=(rows // TOKEN_ROWS,),...  28.8 us
    pallas_call x1, Pallas kernels, finish(): pl.pallas_call(functools.partial(finish_kernel, limit, rate), name='finis...  5.23 us

commit v1 on v0

--- a/solution.py
+++ b/solution.py
@@ -18,7 +18,7 @@
 QUERY_ROWS = 256
 FORWARD_CHUNKS = 1
 KEY_ROWS = 256
-FF_PART = 256
+FF_PART = 1024
 TOKEN_ROWS = 512
 
 F32 = jnp.float32

time: 199 us -> 199 us (level)
  no operation moved by 1% of the time
where the time goes in v1:
time: 199 us; the launch traced here: 200 us
  Pallas kernels  199 us (100%)
    pallas_call x1, Pallas kernels, backward(): pl.pallas_call(functools.partial(backward_kernel, far_count, counts, 1.0...  113 us
    pallas_call x1, Pallas kernels, front(): pl.pallas_call(functools.partial(front_kernel, far_count), name='front',...  52.4 us
    pallas_call x1, Pallas kernels, middle(): pl.pallas_call(middle_kernel, name='middle', grid=(rows // TOKEN_ROWS,),...  28.5 us
    pallas_call x1, Pallas kernels, finish(): pl.pallas_call(functools.partial(finish_kernel, limit, rate), name='finis...  5.23 us

profile of v1, /device:TPU:0, one launch (start us, length us, event | category | flops | bytes accessed | tf_op | source)
XLA Modules:
  0.0 200.1 jit_solution(4963361124549085993)
XLA Ops:
  0.7 52.4 %front.1 = (f32[1024,512]{1,0:T(8,128)}, bf16[1024,512]{1,0:T(8,128)(2,1)}, bf16[2048,128]{1,0:T(8,128)(2,1)}, bf16[3,4,2,64,512]{4,3,2,1,0:T(8,128)(2,1)}, bf16...) custom-call(bf16[1024,512]{1,0:T(8,128)(2,1)} %own_any_states.1, ...), custom_call_target="tpu_custom_call" | custom-call | tf_op jit(solution)/shard_map/front/pallas_call | solution.py:657
  53.0 28.5 %middle.1 = (bf16[1024,512]{1,0:T(8,128)(2,1)}, bf16[1024,512]{1,0:T(8,128)(2,1)}, bf16[1024,512]{1,0:T(8,128)(2,1)}, f32[1024,512]{1,0:T(8,128)}, f32[8,512]{1,...) custom-call(f32[1024,512]{1,0:T(8,128)} %get-tuple-element.69.mixed_ref, ...), custom_call_target="tpu_custom_call" | custom-call | tf_op jit(solution)/shard_map/middle/pallas_call | solution.py:1429
  81.6 113.1 %backward.1 = (f32[64,512]{1,0:T(8,128)}, f32[256,128]{1,0:T(8,128)}, f32[64,128]{1,0:T(8,128)}, f32[8,512]{1,0:T(8,128)}, f32[3,64,128]{2,1,0:T(8,128)}, /*inde...) custom-call(bf16[1024,512]{1,0:T(8,128)(2,1)} %get-tuple-element.74., ...), custom_call_target="tpu_custom_call" | custom-call | tf_op jit(solution)/shard_map/backward/pallas_call | solution.py:1176
  194.7 5.2 %finish.1 = (bf16[1024,512]{1,0:T(8,128)(2,1)}, f32[1,1]{1,0:T(1,128)}, f32[4,64,128]{2,1,0:T(8,128)}, f32[64,512]{1,0:T(8,128)}, f32[256,128]{1,0:T(8,128)}, /*...) custom-call(f32[8,128]{1,0:T(8,128)} %get-tuple-element.88.squares_r, ...), custom_call_target="tpu_custom_call" | custom-call | tf_op jit(solution)/shard_map/finish/pallas_call | solution.py:1263
